TPU v7x, 512 devices: a whole 4x4x16 slice. The times are simulated.
512 devices in a mesh: gx: 64 (over z_lo, x, core), yz: 8 (over y, z_hi).
Axes of the slice: x: 4, y: 4, z: 16 (z_hi: 2, z_lo: 8; z = z_hi * 8 + z_lo), core: 2. Of those that a mesh axis runs over, the one named last changes fastest.
Arguments:
- solution: float32 [4, 512, 64, 3, 128], P(None, 'gx', 'yz'), may hold values from -6 to 6
- residual: float32 [4, 512, 64, 3, 128], P(None, 'gx', 'yz'), may hold values from -6 to 6
- direction: float32 [4, 512, 64, 3, 128], P(None, 'gx', 'yz'), may hold values from -6 to 6
- stiffness: float32 [512, 64, 128], P('gx', 'yz'), may hold values from 0.5 to 13.52
- coupling: float32 [512, 64, 128], P('gx', 'yz'), may hold values from 0.5 to 2
- lower_factor: float32 [64, 8, 384, 384], P('gx', 'yz'), may hold values from -0.122474487 to 1
- upper_factor: float32 [64, 8, 384, 384], P('gx', 'yz'), may hold values from -0.122474487 to 2, as said below
- pivot_order: int32 [64, 8, 384], P('gx', 'yz'), may hold values from 0 to 383, each once within a row
- coarse_basis: float32 [4, 512, 64, 128], P(None, 'gx', 'yz'), may hold values from 0.2 to 1
- coarse_inverse: float32 [64, 8, 12, 6144], P('gx', 'yz'), may hold values from -0.00024917498 to 0.009765625
- inner_prior: float32 [4], replicated, may hold values from 6291456 to 25165824
Outputs:
- solution_next: float32 [4, 512, 64, 3, 128], P(None, 'gx', 'yz')
- residual_next: float32 [4, 512, 64, 3, 128], P(None, 'gx', 'yz')
- direction_next: float32 [4, 512, 64, 3, 128], P(None, 'gx', 'yz')
- inner_next: float32 [4], replicated
Inputs may be any that keep to these rules, and one draw needn't show every extreme that they name: `upper_factor`: upper triangular with positive diagonal.
All inputs are finite; a program needn't handle non-finite values.
Results may differ from a plain program's by a relative error of at most 0.000067.
Values sent between devices are 32-bit elements; how exact they have to be, the bound alone decides.
No kernel may reach another device: no remote copies, remote signals or barrier semaphores. Data moves between devices by JAX's collectives and lax.ppermute only.
A program may use at most 64 MiB of HBM per device.

v0:
```python
import jax
import jax.numpy as jnp
from jax import lax
from jax.sharding import PartitionSpec as P

precise = lax.Precision.HIGHEST


def with_halo(cells, sides, width):
    for axis, dim in sides:
        count = lax.axis_size(axis)
        ends = count - 1
        head = lax.slice_in_dim(cells, 0, width, axis=dim)
        tail = lax.slice_in_dim(cells, cells.shape[dim] - width, cells.shape[dim], axis=dim)
        cells = jnp.concatenate(
            [
                lax.ppermute(tail, axis, [(i, (i + 1) % count) for i in range(ends)]),
                cells,
                lax.ppermute(head, axis, [((i + 1) % count, i) for i in range(ends)]),
            ],
            axis=dim,
        )
    return cells


def stencil(padded, scaled):
    zero_plane = jnp.zeros_like(scaled[..., :1])
    upward = jnp.concatenate([scaled[..., 1:], zero_plane], axis=4)
    downward = jnp.concatenate([zero_plane, scaled[..., :-1]], axis=4)
    beside = padded[:, 2:, 1:-1] + padded[:, :-2, 1:-1] + padded[:, 1:-1, 2:] + padded[:, 1:-1, :-2]
    return 6.0 * scaled - beside - upward - downward


def operate(direction, stiffness, coupling):
    scaled = stiffness[None, :, :, None, :] * direction
    padded = with_halo(scaled, (("gx", 1), ("yz", 2)), 1)
    return stiffness[None, :, :, None, :] * stencil(padded, scaled) + coupling[
        None, :, :, None, :
    ] * jnp.sum(direction, axis=3, keepdims=True)


def local_solve(field, lower_factor, upper_factor, pivot_order):
    line_width = lower_factor.shape[-1]
    line_rows = field.reshape(-1, line_width)
    pivots = pivot_order.reshape(line_width)
    inverse_order = jnp.argsort(pivots)
    permuted = jnp.take(line_rows, pivots, axis=1)
    middle = jnp.dot(
        permuted, lower_factor[0, 0].T, precision=precise, preferred_element_type=jnp.float32
    )
    solved = jnp.dot(
        middle, upper_factor[0, 0].T, precision=precise, preferred_element_type=jnp.float32
    )
    return jnp.take(solved, inverse_order, axis=1).reshape(field.shape)


def across(padded, field):
    field_shape = field.shape
    blank_rows = jnp.zeros(field_shape[:1] + (field_shape[1] - 2,) + field_shape[2:], field.dtype)
    across_first = jnp.concatenate([padded[:, :1, 1:-1], blank_rows, padded[:, -1:, 1:-1]], axis=1)
    blank_cols = jnp.zeros(field_shape[:2] + (field_shape[2] - 2,) + field_shape[3:], field.dtype)
    across_second = jnp.concatenate([padded[:, 1:-1, :1], blank_cols, padded[:, 1:-1, -1:]], axis=2)
    return field + 0.5 * (across_first + across_second)


def restrict(coarse_basis, field):
    weighted = jnp.einsum("pxyz,cxykz->ckp", coarse_basis, field, precision=precise)
    return weighted.reshape(field.shape[0], -1)


def prolong(coarse_basis, coarse_values, field_shape):
    shaped = coarse_values.reshape(field_shape[0], field_shape[3], coarse_basis.shape[0])
    return jnp.einsum("pxyz,ckp->cxykz", coarse_basis, shaped, precision=precise)


def per_device(
    solution,
    residual,
    direction,
    stiffness,
    coupling,
    lower_factor,
    upper_factor,
    pivot_order,
    coarse_basis,
    coarse_inverse,
    inner_prior,
):
    case_count = residual.shape[0]
    applied = operate(direction, stiffness, coupling)
    curve_part = jnp.sum(direction * applied, axis=(1, 2, 3, 4))
    curvature = lax.psum(curve_part, ("gx", "yz"))
    step_size = inner_prior / curvature
    step_field = step_size[:, None, None, None, None]
    residual_next = residual - step_field * applied
    primal = restrict(coarse_basis, residual_next)
    primal_all = lax.all_gather(primal[:, None, :], ("gx", "yz"), axis=1, tiled=True).reshape(
        case_count, -1
    )
    coarse_values = jnp.dot(
        primal_all, coarse_inverse[0, 0].T, precision=precise, preferred_element_type=jnp.float32
    )
    correction = prolong(coarse_basis, coarse_values, residual.shape)
    local_part = local_solve(residual_next, lower_factor, upper_factor, pivot_order)
    padded = with_halo(local_part, (("gx", 1), ("yz", 2)), 1)
    smoothed = across(padded, local_part)
    preconditioned = smoothed + correction
    inner_part = jnp.sum(residual_next * preconditioned, axis=(1, 2, 3, 4))
    inner_next = lax.psum(inner_part, ("gx", "yz"))
    growth = (inner_next / inner_prior)[:, None, None, None, None]
    direction_next = preconditioned + growth * direction
    solution_next = solution + step_field * direction
    return (solution_next, residual_next, direction_next, inner_next)


def solution(mesh):
    in_specs = (
        P(None, "gx", "yz", None, None),
        P(None, "gx", "yz", None, None),
        P(None, "gx", "yz", None, None),
        P("gx", "yz", None),
        P("gx", "yz", None),
        P("gx", "yz", None, None),
        P("gx", "yz", None, None),
        P("gx", "yz", None),
        P(None, "gx", "yz", None),
        P("gx", "yz", None, None),
        P(),
    )
    out_specs = (
        P(None, "gx", "yz", None, None),
        P(None, "gx", "yz", None, None),
        P(None, "gx", "yz", None, None),
        P(),
    )
    return jax.shard_map(
        per_device, mesh=mesh, in_specs=in_specs, out_specs=out_specs, check_vma=False
    )
```

profile of v0, /device:TPU:1, one launch (start us, length us, event | category | flops | bytes accessed | tf_op | source)
XLA Modules:
  0.0 2391.1 jit_solution(16158936149588700655)
XLA Ops:
  0.6 0.0 copy-start
  0.6 1.3 copy_multiply_fusion
  2.0 8.7 collective-permute-start
  10.8 0.0 copy-start.10
  10.8 0.0 copy-start.1
  10.8 2.1 collective-permute-start.1
  12.8 0.3 fusion.30
  13.1 0.0 copy-done.10
  13.2 0.0 copy-done.1
  13.2 0.0 copy-start.9
  13.2 0.0 copy-start.6
  13.2 3.8 sort.17
  17.0 0.0 copy-done.9
  17.1 0.1 copy.50
  17.1 0.0 copy-done.6
  17.2 0.7 reduce.1
  17.9 0.1 dot_general.20
  18.0 0.1 pad.6.clone
  18.0 0.0 collective-permute-done
  18.1 0.0 collective-permute-done.1
  18.1 11.2 collective-permute-start.3
  29.3 1.3 collective-permute-start.2
  30.6 3.7 collective-permute-done.3
  34.3 10.0 collective-permute-done.2
  44.3 0.0 copy-done.7
  44.3 0.7 multiply_reduce_fusion.1
  45.0 103.4 %psum.14 = f32[4]{0:T(128)S(1)} all-reduce(f32[4]{0:T(128)S(1)} %get-tuple-element.19), channel_id=1, replica_groups=mesh['gx'=64,'yz'=8] {'gx','yz'}, use_global_device_ids=true, to_apply=%region_2.0 | all-reduce | flops 4 | bytes 32 | tf_op jit(solution)/shard_map/psum | solution.py:92
  148.5 0.0 copy-done.11
  148.5 0.0 copy-done.5
  148.5 0.3 copy_subtract_fusion
  148.8 0.0 copy-start.8
  148.9 0.0 copy-start.2
  148.9 0.8 copy-done.8
  149.7 1.6 convolution_bitcast_fusion.1
  151.3 0.1 broadcast_in_dim_reshape.3
  151.4 0.2 copy.56
  151.6 0.0 copy-done.2
  151.6 1.7 gather_fusion
  153.3 0.0 copy-start.3
  153.3 1.5 fusion.2
  154.8 0.8 fusion
  155.6 1.7 gather_fusion.1
  157.3 0.1 select_bitcast_fusion
  157.4 0.2 copy.58
  157.6 2.6 collective-permute-start.4
  160.2 2047.1 %all_gather.3 = f32[4,512,12]{2,0,1:T(4,128)S(1)} all-gather(f32[4,1,12]{2,0,1:T(4,128)S(1)} %broadcast_in_dim_reshape.3), channel_id=1, replica_groups=mesh['gx'=64,'yz'=8] {'gx','yz'}, dimensions={1}, use_global_device_ids=true | all-gather | bytes 98496 | tf_op jit(solution)/shard_map/all_gather | solution.py:97
  2207.3 0.1 copy.66
  2207.4 0.7 reshape.66
  2208.1 1.9 collective-permute-start.5
  2210.0 0.0 collective-permute-done.4
  2210.1 0.3 constant_dynamic-update-slice_fusion.1
  2210.4 15.4 collective-permute-done.5
  2225.8 1.3 collective-permute-start.7
  2227.1 12.9 collective-permute-start.6
  2240.0 3.3 convolution_bitcast_fusion.2
  2243.2 0.0 collective-permute-done.7
  2243.3 0.0 collective-permute-done.6
  2243.3 0.0 copy-start.4
  2243.3 1.0 multiply_reduce_fusion
  2244.3 144.2 %psum.15 = f32[4]{0:T(128)S(1)} all-reduce(f32[4]{0:T(128)S(1)} %get-tuple-element.33), channel_id=1, replica_groups=mesh['gx'=64,'yz'=8] {'gx','yz'}, use_global_device_ids=true, to_apply=%region_5.7 | all-reduce | flops 4 | bytes 32 | tf_op jit(solution)/shard_map/psum | solution.py:109
  2388.5 0.5 copy-done.12
  2389.0 0.6 multiply_add_fusion
  2389.6 0.8 copy.69
  2390.4 0.8 copy.71
  (31 shorter events, 0.3 us)
Async XLA Ops:
  0.6 152.6 %copy-start = (f32[1,1,384,384]{3,2,1,0:T(8,128)S(1)}, f32[1,1,384,384]{3,2,1,0:T(8,128)}, u32[]{:S(2)}) copy-start(f32[1,1,384,384]{3,2,1,0:T(8,128)} %param.18) | copy-start | bytes 1769476
  2.0 16.1 collective-permute-start
  10.8 2.4 copy-start.10
  10.8 2.4 copy-start.1
  10.8 7.3 collective-permute-start.1
  13.2 3.8 copy-start.9
  13.2 3.9 copy-start.6
  18.1 26.2 %copy-start.7 = (f32[8,8,128]{2,1,0:T(8,128)S(1)}, f32[8,8,128]{2,1,0:T(8,128)}, u32[]{:S(2)}) copy-start(f32[8,8,128]{2,1,0:T(8,128)} %param.16) | copy-start | bytes 98308
  18.1 16.2 collective-permute-start.3
  29.3 15.0 collective-permute-start.2
  44.3 104.2 %copy-start.5 = (f32[4,8,8,3,128]{4,2,3,1,0:T(8,128)S(1)}, f32[4,8,8,3,128]{4,2,3,1,0:T(8,128)}, u32[]{:S(2)}) copy-start(f32[4,8,8,3,128]{4,2,3,1,0:T(8,128)} %param.14) | copy-start | bytes 1179652
  45.0 103.5 %copy-start.11 = (f32[4]{0:T(128)S(1)}, f32[4]{0:T(128)}, u32[]{:S(2)}) copy-start(f32[4]{0:T(128)} %param.23) | copy-start | bytes 52
  148.8 0.9 copy-start.8
  148.9 2.7 copy-start.2
  153.3 1.5 copy-start.3
  157.6 2052.4 %collective-permute-start.4 = (f32[4,1,8,3,128]{4,0,2,1,3:T(4,128)S(1)}, f32[4,1,8,3,128]{4,0,2,1,3:T(4,128)S(1)}, u32[]{:S(2)}, u32[]{:S(2)}) collective-permute-start(f32[4,1,8,3,128]{4,0,2,1,3:T(4,128)S(1)} %copy.96), channel_id=1, source_target_pairs={{0,8},{8,16},{16,24},{24,32},{32,40},{40,48},{48,56},{56,64},{64,7... | collective-permute-start | bytes 147464 | tf_op jit(solution)/shard_map/ppermute | solution.py:17
  2208.1 17.6 collective-permute-start.5
  2225.8 17.5 collective-permute-start.7
  2227.1 16.2 collective-permute-start.6
  2243.3 145.7 %copy-start.4 = (f32[4,8,8,3,128]{4,2,3,1,0:T(8,128)S(1)}, f32[4,8,8,3,128]{4,2,3,1,0:T(8,128)}, u32[]{:S(2)}) copy-start(f32[4,8,8,3,128]{4,2,3,1,0:T(8,128)} %param.13) | copy-start | bytes 1179652
  2388.5 0.5 copy-start.12
where the time goes:
time: 2390 us
  blocking collectives  2290 us (96%)
  starting transfers between devices  42 us (2%)
  waiting for transfers between devices  29.1 us (1%)
    all_gather x1, blocking collectives, per_device(): lax.all_gather(primal[:, None, :], ('gx', 'yz'), axis=1, tiled=True)  2050 us
    psum x1, blocking collectives, per_device(): inner_next = lax.psum(inner_part, ('gx', 'yz'))  144 us
    psum x1, blocking collectives, per_device(): curvature = lax.psum(curve_part, ('gx', 'yz'))  103 us
  transfers between devices with their start and end apart: 8, of which 3 were waited for; matrix products, arithmetic and copies ran while one was open for 0% of the time, Pallas kernels for 0%

commit v1 on v0

--- a/solution.py
+++ b/solution.py
@@ -4,6 +4,13 @@
 from jax.sharding import PartitionSpec as P
 
 precise = lax.Precision.HIGHEST
+
+
+def all_by_exchange(array, axis, dim):
+    peers = lax.axis_size(axis)
+    tiles = jnp.stack([array for _ in range(peers)])
+    tiles = lax.all_to_all(tiles, axis, split_axis=0, concat_axis=0)
+    return jnp.concatenate(tiles, axis=dim)
 
 
 def with_halo(cells, sides, width):
@@ -94,9 +101,7 @@
     step_field = step_size[:, None, None, None, None]
     residual_next = residual - step_field * applied
     primal = restrict(coarse_basis, residual_next)
-    primal_all = lax.all_gather(primal[:, None, :], ("gx", "yz"), axis=1, tiled=True).reshape(
-        case_count, -1
-    )
+    primal_all = all_by_exchange(primal[:, None, :], ("gx", "yz"), 1).reshape(case_count, -1)
     coarse_values = jnp.dot(
         primal_all, coarse_inverse[0, 0].T, precision=precise, preferred_element_type=jnp.float32
     )

time: 2390 us -> 363 us (0.15)
  blocking collectives: 2290 us -> 225 us
    all_gather x1 -> x0, blocking collectives: 2050 us -> none  [per_device(): lax.all_gather(primal[:, None, :], ('gx', 'yz'), axis=1, tiled=True)]
  transfers between devices with their start and end apart: 8 -> 9, of which waited for: 3 -> 4; matrix products, arithmetic and copies ran while one was open for 0% -> 2% of each run, Pallas kernels for 0% -> 0%
where the time goes in v1:
time: 363 us; the launch traced here: 362 us
  blocking collectives  225 us (62%)
  starting transfers between devices  60.2 us (17%)
  waiting for transfers between devices  48 us (13%)
  local copies, waits for them, and re-layouts  11.6 us (3%)
  matrix products  8.19 us (2%)
  other arithmetic  7.68 us (2%)
    psum x1, blocking collectives, per_device(): inner_next = lax.psum(inner_part, ('gx', 'yz'))  122 us
    psum x1, blocking collectives, per_device(): curvature = lax.psum(curve_part, ('gx', 'yz'))  104 us
    ppermute x4, waiting for transfers between devices, with_halo(): lax.ppermute(head, axis, [((i + 1) % count, i) for i in range(ends)])  44.3 us
    ppermute x4, starting transfers between devices, with_halo(): lax.ppermute(tail, axis, [(i, (i + 1) % count) for i in range(ends)])  29 us
    ppermute x4, starting transfers between devices, with_halo(): lax.ppermute(head, axis, [((i + 1) % count, i) for i in range(ends)])  17.5 us
    all_to_all x1, starting transfers between devices, all_by_exchange(): tiles = lax.all_to_all(tiles, axis, split_axis=0, concat_axis=0)  13.7 us
  transfers between devices with their start and end apart: 9, of which 4 were waited for; matrix products, arithmetic and copies ran while one was open for 2% of the time, Pallas kernels for 0%

profile of v1, /device:TPU:1, one launch (start us, length us, event | category | flops | bytes accessed | tf_op | source)
XLA Modules:
  0.0 362.1 jit_solution(15280283728341117921)
XLA Ops:
  0.6 0.0 copy-start
  0.6 1.3 copy_multiply_fusion
  2.0 8.7 %collective-permute-start = (f32[4,1,8,3,128]{4,0,2,1,3:T(4,128)S(1)}, f32[4,1,8,3,128]{4,0,2,1,3:T(4,128)S(1)}, u32[]{:S(2)}, u32[]{:S(2)}) collective-permute-start(f32[4,1,8,3,128]{4,0,2,1,3:T(4,128)S(1)} %get-tuple-element.30), channel_id=1, source_target_pairs={{8,0},{16,8},{24,16},{32,24},{40,32},{48,40},{56,48},{64,56},{72,6... | collective-permute-start | bytes 147464 | tf_op jit(solution)/shard_map/ppermute | solution.py:26
  10.8 0.0 copy-start.17
  10.8 0.0 copy-start.1
  10.8 2.1 collective-permute-start.1
  12.8 0.3 fusion.30
  13.2 0.0 copy-start.16
  13.2 3.8 %sort.17 = (s32[384]{0:T(512)}, s32[384]{0:T(512)S(1)}) sort(s32[384]{0:T(512)S(1)} %reduce, s32[384]{0:T(512)S(1)} %iota.4), dimensions={0}, to_apply=%region_3.5 | sort | flops 3456 | bytes 6144 | tf_op jit(solution)/shard_map/jit(argsort)/sort | solution.py:53
  17.0 0.1 copy.49
  17.2 0.0 copy-start.12
  17.2 11.2 %collective-permute-start.3 = (f32[4,10,1,3,128]{4,0,2,1,3:T(4,128)S(1)}, f32[4,10,1,3,128]{4,0,2,1,3:T(4,128)S(1)}, u32[]{:S(2)}, u32[]{:S(2)}) collective-permute-start(f32[4,10,1,3,128]{4,0,2,1,3:T(4,128)S(1)} %get-tuple-element.24), channel_id=1, source_target_pairs={{0,1},{1,2},{2,3},{3,4},{4,5},{5,6},{6,7},{8,9},{9,10},{10,11},{11... | collective-permute-start | bytes 184328 | tf_op jit(solution)/shard_map/ppermute | solution.py:24
  28.4 1.3 collective-permute-start.2
  29.7 3.7 %collective-permute-done.3 = f32[4,10,1,3,128]{4,0,2,1,3:T(4,128)S(1)} collective-permute-done((f32[4,10,1,3,128]{4,0,2,1,3:T(4,128)S(1)}, f32[4,10,1,3,128]{4,0,2,1,3:T(4,128)S(1)}, u32[]{:S(2)}, u32[]{:S(2)}) %collective-permute-start.3) | collective-permute-done | bytes 61472 | tf_op jit(solution)/shard_map/ppermute | solution.py:24
  33.4 10.4 %collective-permute-done.2 = f32[4,10,1,3,128]{4,0,2,1,3:T(4,128)S(1)} collective-permute-done((f32[4,10,1,3,128]{4,0,2,1,3:T(4,128)S(1)}, f32[4,10,1,3,128]{4,0,2,1,3:T(4,128)S(1)}, u32[]{:S(2)}, u32[]{:S(2)}) %collective-permute-start.2) | collective-permute-done | bytes 61472 | tf_op jit(solution)/shard_map/ppermute | solution.py:26
  43.9 0.7 multiply_reduce_fusion.1
  44.6 103.7 %psum.14 = f32[4]{0:T(128)S(1)} all-reduce(f32[4]{0:T(128)S(1)} %get-tuple-element.19), channel_id=1, replica_groups=mesh['gx'=64,'yz'=8] {'gx','yz'}, use_global_device_ids=true, to_apply=%region_2.0 | all-reduce | flops 4 | bytes 32 | tf_op jit(solution)/shard_map/psum | solution.py:99
  148.4 0.3 copy_subtract_fusion
  148.7 0.0 copy-start.2
  148.7 0.0 copy-start.6
  148.8 0.2 copy.55
  148.9 0.6 copy-done.6
  149.6 1.7 gather_fusion
  151.2 0.0 copy-start.8
  151.2 1.5 fusion.2
  152.8 0.8 fusion
  153.6 1.7 gather_fusion.1
  155.3 0.1 select_bitcast_fusion
  155.4 0.2 copy.57
  155.5 0.0 copy-start.4
  155.6 0.0 copy-start.13
  155.6 2.1 collective-permute-start.4
  157.7 1.6 convolution_bitcast_fusion.1
  159.3 0.1 stack_broadcast_in_dim_reshape.2
  159.4 1.1 stack.3
  160.5 13.7 %all-to-all-start = ((f32[512,4,1,12]{3,1,2,0:T(4,128)}), f32[512,4,1,12]{3,1,2,0:T(4,128)S(1)}, u32[]{:S(2)}, u32[]{:S(2)}) async-start(f32[512,4,1,12]{3,1,2,0:T(4,128)} %stack.3), calls=%async_computation | async-start | bytes 2097152 | tf_op jit(solution)/shard_map/all_to_all | solution.py:12
  174.2 6.2 %collective-permute-start.5 = (f32[4,1,8,3,128]{4,0,2,1,3:T(4,128)S(1)}, f32[4,1,8,3,128]{4,0,2,1,3:T(4,128)S(1)}, u32[]{:S(2)}, u32[]{:S(2)}) collective-permute-start(f32[4,1,8,3,128]{4,0,2,1,3:T(4,128)S(1)} %copy.94), channel_id=1, source_target_pairs={{8,0},{16,8},{24,16},{32,24},{40,32},{48,40},{56,48},{64,56},{72,6... | collective-permute-start | bytes 147464 | tf_op jit(solution)/shard_map/ppermute | solution.py:26
  180.5 0.3 constant_dynamic-update-slice_fusion.1
  180.8 0.0 copy-start.11
  180.8 0.5 collective-permute-done.5
  181.3 1.3 collective-permute-start.7
  182.6 13.7 %collective-permute-start.6 = (f32[4,10,1,3,128]{4,0,2,1,3:T(4,128)S(1)}, f32[4,10,1,3,128]{4,0,2,1,3:T(4,128)S(1)}, u32[]{:S(2)}, u32[]{:S(2)}) collective-permute-start(f32[4,10,1,3,128]{4,0,2,1,3:T(4,128)S(1)} %get-tuple-element.21), channel_id=1, source_target_pairs={{0,1},{1,2},{2,3},{3,4},{4,5},{5,6},{6,7},{8,9},{9,10},{10,11},{11... | collective-permute-start | bytes 184328 | tf_op jit(solution)/shard_map/ppermute | solution.py:24
  196.3 0.7 reduce.1
  197.0 0.8 dot_general.20
  197.9 0.1 pad.6.clone
  197.9 33.4 %collective-permute-done.7 = f32[4,10,1,3,128]{4,0,2,1,3:T(4,128)S(1)} collective-permute-done((f32[4,10,1,3,128]{4,0,2,1,3:T(4,128)S(1)}, f32[4,10,1,3,128]{4,0,2,1,3:T(4,128)S(1)}, u32[]{:S(2)}, u32[]{:S(2)}) %collective-permute-start.7) | collective-permute-done | bytes 61472 | tf_op jit(solution)/shard_map/ppermute | solution.py:26
  231.3 0.6 copy-done.14
  231.9 0.0 collective-permute-done.6
  231.9 0.6 copy-done.15
  232.6 0.0 all-to-all-done
  232.6 0.1 copy.65
  232.6 0.0 copy-start.5
  232.7 0.0 slice-start
  232.7 0.7 reshape.70
  233.4 0.2 copy-done.7
  233.6 3.3 convolution_bitcast_fusion.2
  236.9 0.0 copy-done.3
  236.9 0.0 copy-start.9
  236.9 1.0 multiply_reduce_fusion
  238.0 121.5 %psum.15 = f32[4]{0:T(128)S(1)} all-reduce(f32[4]{0:T(128)S(1)} %get-tuple-element.33), channel_id=1, replica_groups=mesh['gx'=64,'yz'=8] {'gx','yz'}, use_global_device_ids=true, to_apply=%region_5.7 | all-reduce | flops 4 | bytes 32 | tf_op jit(solution)/shard_map/psum | solution.py:114
  359.5 0.5 copy-done.19
  360.0 0.6 multiply_add_fusion
  360.6 0.8 copy.68
  361.3 0.8 copy.70
  (49 shorter events, 0.3 us)
Async XLA Ops:
  0.6 150.6 %copy-start = (f32[1,1,384,384]{3,2,1,0:T(8,128)S(1)}, f32[1,1,384,384]{3,2,1,0:T(8,128)}, u32[]{:S(2)}) copy-start(f32[1,1,384,384]{3,2,1,0:T(8,128)} %param.18) | copy-start | bytes 1769476
  2.0 15.1 %collective-permute-start = (f32[4,1,8,3,128]{4,0,2,1,3:T(4,128)S(1)}, f32[4,1,8,3,128]{4,0,2,1,3:T(4,128)S(1)}, u32[]{:S(2)}, u32[]{:S(2)}) collective-permute-start(f32[4,1,8,3,128]{4,0,2,1,3:T(4,128)S(1)} %get-tuple-element.30), channel_id=1, source_target_pairs={{8,0},{16,8},{24,16},{32,24},{40,32},{48,40},{56,48},{64,56},{72,6... | collective-permute-start | bytes 147464 | tf_op jit(solution)/shard_map/ppermute | solution.py:26
  10.8 2.4 copy-start.17
  10.8 2.4 copy-start.1
  10.8 6.4 %collective-permute-start.1 = (f32[4,1,8,3,128]{4,0,2,1,3:T(4,128)S(1)}, f32[4,1,8,3,128]{4,0,2,1,3:T(4,128)S(1)}, u32[]{:S(2)}, u32[]{:S(2)}) collective-permute-start(f32[4,1,8,3,128]{4,0,2,1,3:T(4,128)S(1)} %get-tuple-element.29), channel_id=1, source_target_pairs={{0,8},{8,16},{16,24},{24,32},{32,40},{40,48},{48,56},{56,64},{64,7... | collective-permute-start | bytes 147464 | tf_op jit(solution)/shard_map/ppermute | solution.py:24
  13.2 3.8 %copy-start.16 = (f32[8,8,128]{2,1,0:T(8,128)S(1)}, f32[8,8,128]{2,1,0:T(8,128)}, u32[]{:S(2)}) copy-start(f32[8,8,128]{2,1,0:T(8,128)} %param.17) | copy-start | bytes 98308
  17.2 26.7 %copy-start.12 = (f32[8,8,128]{2,1,0:T(8,128)S(1)}, f32[8,8,128]{2,1,0:T(8,128)}, u32[]{:S(2)}) copy-start(f32[8,8,128]{2,1,0:T(8,128)} %param.16) | copy-start | bytes 98308
  17.2 16.2 %collective-permute-start.3 = (f32[4,10,1,3,128]{4,0,2,1,3:T(4,128)S(1)}, f32[4,10,1,3,128]{4,0,2,1,3:T(4,128)S(1)}, u32[]{:S(2)}, u32[]{:S(2)}) collective-permute-start(f32[4,10,1,3,128]{4,0,2,1,3:T(4,128)S(1)} %get-tuple-element.24), channel_id=1, source_target_pairs={{0,1},{1,2},{2,3},{3,4},{4,5},{5,6},{6,7},{8,9},{9,10},{10,11},{11... | collective-permute-start | bytes 184328 | tf_op jit(solution)/shard_map/ppermute | solution.py:24
  28.4 15.5 %collective-permute-start.2 = (f32[4,10,1,3,128]{4,0,2,1,3:T(4,128)S(1)}, f32[4,10,1,3,128]{4,0,2,1,3:T(4,128)S(1)}, u32[]{:S(2)}, u32[]{:S(2)}) collective-permute-start(f32[4,10,1,3,128]{4,0,2,1,3:T(4,128)S(1)} %get-tuple-element.23), channel_id=1, source_target_pairs={{1,0},{2,1},{3,2},{4,3},{5,4},{6,5},{7,6},{9,8},{10,9},{11,10},{12... | collective-permute-start | bytes 184328 | tf_op jit(solution)/shard_map/ppermute | solution.py:26
  43.9 104.5 %copy-start.10 = (f32[4,8,8,3,128]{4,2,3,1,0:T(8,128)S(1)}, f32[4,8,8,3,128]{4,2,3,1,0:T(8,128)}, u32[]{:S(2)}) copy-start(f32[4,8,8,3,128]{4,2,3,1,0:T(8,128)} %param.14) | copy-start | bytes 1179652
  44.6 103.8 %copy-start.18 = (f32[4]{0:T(128)S(1)}, f32[4]{0:T(128)}, u32[]{:S(2)}) copy-start(f32[4]{0:T(128)} %param.23) | copy-start | bytes 52
  148.7 9.0 %copy-start.2 = (f32[4,8,8,3,128]{4,0,2,1,3:T(4,128)}, f32[4,8,8,3,128]{4,0,2,1,3:T(4,128)S(1)}, u32[]{:S(2)}) copy-start(f32[4,8,8,3,128]{4,0,2,1,3:T(4,128)S(1)} %copy_subtract_fusion) | copy-start | bytes 1179652
  148.7 0.8 copy-start.6
  151.2 1.5 copy-start.8
  155.5 24.9 %copy-start.4 = (f32[256,384]{1,0:T(8,128)}, f32[256,384]{1,0:T(8,128)S(1)}, u32[]{:S(2)}) copy-start(f32[256,384]{1,0:T(8,128)S(1)} %copy.57) | copy-start | bytes 1179652
  155.6 2.1 copy-start.13
  155.6 24.8 %collective-permute-start.4 = (f32[4,1,8,3,128]{4,0,2,1,3:T(4,128)S(1)}, f32[4,1,8,3,128]{4,0,2,1,3:T(4,128)S(1)}, u32[]{:S(2)}, u32[]{:S(2)}) collective-permute-start(f32[4,1,8,3,128]{4,0,2,1,3:T(4,128)S(1)} %copy.95), channel_id=1, source_target_pairs={{0,8},{8,16},{16,24},{24,32},{32,40},{40,48},{48,56},{56,64},{64,7... | collective-permute-start | bytes 147464 | tf_op jit(solution)/shard_map/ppermute | solution.py:24
  160.5 72.1 %all-to-all-start = ((f32[512,4,1,12]{3,1,2,0:T(4,128)}), f32[512,4,1,12]{3,1,2,0:T(4,128)S(1)}, u32[]{:S(2)}, u32[]{:S(2)}) async-start(f32[512,4,1,12]{3,1,2,0:T(4,128)} %stack.3), calls=%async_computation | async-start | bytes 2097152 | tf_op jit(solution)/shard_map/all_to_all | solution.py:12
  174.2 7.1 %collective-permute-start.5 = (f32[4,1,8,3,128]{4,0,2,1,3:T(4,128)S(1)}, f32[4,1,8,3,128]{4,0,2,1,3:T(4,128)S(1)}, u32[]{:S(2)}, u32[]{:S(2)}) collective-permute-start(f32[4,1,8,3,128]{4,0,2,1,3:T(4,128)S(1)} %copy.94), channel_id=1, source_target_pairs={{8,0},{16,8},{24,16},{32,24},{40,32},{48,40},{56,48},{64,56},{72,6... | collective-permute-start | bytes 147464 | tf_op jit(solution)/shard_map/ppermute | solution.py:26
  180.8 15.6 %copy-start.11 = (f32[1,1,12,6144]{3,1,2,0:T(1,128)S(1)}, f32[1,1,12,6144]{3,1,2,0:T(1,128)}, u32[]{:S(2)}) copy-start(f32[1,1,12,6144]{3,1,2,0:T(1,128)} %param.22) | copy-start | bytes 884740
  181.3 50.0 %collective-permute-start.7 = (f32[4,10,1,3,128]{4,0,2,1,3:T(4,128)S(1)}, f32[4,10,1,3,128]{4,0,2,1,3:T(4,128)S(1)}, u32[]{:S(2)}, u32[]{:S(2)}) collective-permute-start(f32[4,10,1,3,128]{4,0,2,1,3:T(4,128)S(1)} %get-tuple-element.22), channel_id=1, source_target_pairs={{1,0},{2,1},{3,2},{4,3},{5,4},{6,5},{7,6},{9,8},{10,9},{11,10},{12... | collective-permute-start | bytes 184328 | tf_op jit(solution)/shard_map/ppermute | solution.py:26
  182.6 49.3 %collective-permute-start.6 = (f32[4,10,1,3,128]{4,0,2,1,3:T(4,128)S(1)}, f32[4,10,1,3,128]{4,0,2,1,3:T(4,128)S(1)}, u32[]{:S(2)}, u32[]{:S(2)}) collective-permute-start(f32[4,10,1,3,128]{4,0,2,1,3:T(4,128)S(1)} %get-tuple-element.21), channel_id=1, source_target_pairs={{0,1},{1,2},{2,3},{3,4},{4,5},{5,6},{6,7},{8,9},{9,10},{10,11},{11... | collective-permute-start | bytes 184328 | tf_op jit(solution)/shard_map/ppermute | solution.py:24
  231.3 0.6 copy-start.14
  231.9 0.6 copy-start.15
  232.6 1.0 copy-start.7
  232.6 4.2 %copy-start.5 = (f32[256,384]{1,0:T(8,128)S(1)}, f32[256,384]{1,0:T(8,128)}, u32[]{:S(2)}) copy-start(f32[256,384]{1,0:T(8,128)} %copy-done.4) | copy-start | bytes 1179652
  232.7 4.2 %slice-start = ((f32[4,10,1,3,128]{4,0,2,1,3:T(4,128)}), f32[4,8,1,3,128]{4,0,2,1,3:T(4,128)S(1)}, s32[]{:S(2)}) async-start(f32[4,10,1,3,128]{4,0,2,1,3:T(4,128)} %copy-done.14), calls=%async_computation.1 | async-start | bytes 98304 | tf_op jit(solution)/shard_map/slice | solution.py:69
  232.7 4.2 %slice-start.1 = ((f32[4,10,1,3,128]{4,0,2,1,3:T(4,128)}), f32[4,8,1,3,128]{4,0,2,1,3:T(4,128)S(1)}, s32[]{:S(2)}) async-start(f32[4,10,1,3,128]{4,0,2,1,3:T(4,128)} %copy-done.15), calls=%async_computation.2 | async-start | bytes 98304 | tf_op jit(solution)/shard_map/slice | solution.py:69
  233.6 3.3 copy-start.3
  236.9 123.1 %copy-start.9 = (f32[4,8,8,3,128]{4,2,3,1,0:T(8,128)S(1)}, f32[4,8,8,3,128]{4,2,3,1,0:T(8,128)}, u32[]{:S(2)}) copy-start(f32[4,8,8,3,128]{4,2,3,1,0:T(8,128)} %param.13) | copy-start | bytes 1179652
  359.5 0.5 copy-start.19
